TPU v7x, 256 devices: a whole 4x4x8 slice. The times are simulated.
256 devices in a mesh: dp: 4 (over y), seq: 8 (over x, core), tensor: 8 (over z).
Axes of the slice: x: 4, y: 4, z: 8, core: 2. Of those that a mesh axis runs over, the one named last changes fastest.
Arguments:
- tokens: bfloat16 [4, 4096, 8192], P('dp', ('seq', 'tensor')), may hold values from -19 to 19
- norm_gain: float32 [8192], replicated, may hold values from 0.1 to 1.9
- master_weight: float32 [8192, 3, 4096], P(('dp', 'seq'), None, 'tensor'), may hold values from -5 to 5
- short_filter: float32 [3, 3, 4096], P(None, None, 'tensor'), may hold values from -2600 to 2600
- medium_filter: bfloat16 [128, 4096], P(None, 'tensor'), may hold values from -1 to 1
- medium_skip: float32 [4096], P('tensor'), may hold values from 0.5 to 1.5
Outputs:
- mixed: bfloat16 [4, 4096, 4096], P('dp', 'seq', 'tensor')
- weight_amax: float32 [1], replicated
All inputs are finite; a program needn't handle non-finite values.
Results may differ from a plain program's by a relative error of at most 0.015.
Values may be sent and summed in bfloat16 or wider, within the bound.
A program may use at most 128 MiB of HBM per device.

v0:
```python
import jax
import jax.numpy as jnp
from jax import lax
from jax.sharding import PartitionSpec as P

grid_top = 448.0
eps_norm = 1e-06
eps_peak = 1e-06
power_steps = [2.0, 4.0, 16.0, 256.0, 65536.0, 4294967296.0, 1.8446744073709552e19]


def passed_along(x, axis, by):
    length = lax.axis_size(axis)
    pairs = [(i, i + by) for i in range(length) if 0 <= i + by < length]
    return lax.ppermute(x, axis, pairs)


def exact_power(exponent):
    magnitude = jnp.abs(exponent)
    result = jnp.ones(exponent.shape, jnp.float32)
    for bit_place in range(7):
        chosen = magnitude >> bit_place & 1 == 1
        result = result * jnp.where(chosen, power_steps[bit_place], 1.0)
    return jnp.where(exponent >= 0, result, 1.0 / result)


def narrow_grid(entries):
    magnitude = jnp.abs(entries)
    exponent = jnp.floor(jnp.log2(jnp.maximum(magnitude, 1e-30))).astype(jnp.int32)
    quantum = exact_power(jnp.maximum(exponent, -6) - 3)
    return jnp.sign(entries) * jnp.floor(magnitude / quantum + 0.5) * quantum


def short_conv(padded, filters, length, margin):
    summed = jnp.zeros((length,) + padded.shape[1:], jnp.float32)
    for lag_index in range(filters.shape[1]):
        window = padded[margin - lag_index : margin - lag_index + length].astype(jnp.float32)
        summed = summed + filters[:, lag_index, :] * window
    return summed


def shards(tokens, norm_gain, master_weight, short_filter, medium_filter, medium_skip):
    short_taps = short_filter.shape[1]
    medium_taps = medium_filter.shape[0]
    values = tokens.astype(jnp.float32)
    square_mean = jnp.mean(values * values, axis=-1, keepdims=True)
    normed = (values * lax.rsqrt(square_mean + eps_norm) * norm_gain).astype(jnp.bfloat16)
    gathered = lax.all_gather(normed, "tensor", axis=1, tiled=True)
    stacks = gathered.shape[0]
    seq_rows = gathered.shape[1]
    model_width = gathered.shape[2]
    flat_rows = gathered.reshape(stacks * seq_rows, model_width)
    owned_rows = master_weight.shape[0]
    channels = master_weight.shape[2]
    peak_value = lax.pmax(jnp.max(jnp.abs(master_weight)), ("dp", "seq", "tensor"))
    factor = exact_power(jnp.floor(jnp.log2(grid_top / (peak_value + eps_peak))).astype(jnp.int32))
    recast = (
        narrow_grid(master_weight * factor).astype(jnp.bfloat16).reshape(owned_rows, 3 * channels)
    )
    projected = jnp.dot(
        flat_rows,
        lax.all_gather(recast, ("dp", "seq"), axis=0, tiled=True),
        preferred_element_type=jnp.float32,
    )
    features = (projected / factor).astype(jnp.bfloat16).reshape(seq_rows, 3, channels)
    rim_rows = passed_along(features[seq_rows - (short_taps - 1) :], "seq", 1)
    padded = jnp.concatenate([rim_rows, features], axis=0)
    mixed_conv = short_conv(padded, short_filter, seq_rows, short_taps - 1)
    gated = (mixed_conv[:, 1] * mixed_conv[:, 2]).astype(jnp.bfloat16)
    earlier = passed_along(gated[seq_rows - (medium_taps - 1) :], "seq", 1)
    extended = jnp.concatenate([earlier, gated], axis=0)
    post_gate = mixed_conv[:, 0]
    kernel = medium_filter[::-1][:, None, :]
    filtered = lax.conv_general_dilated(
        extended[None],
        kernel,
        (1,),
        "VALID",
        dimension_numbers=("NWC", "WIO", "NWC"),
        feature_group_count=channels,
        preferred_element_type=jnp.float32,
    )[0]
    filtered = filtered + medium_skip * gated.astype(jnp.float32)
    mixed_rows = (post_gate * filtered).astype(jnp.bfloat16)
    return (mixed_rows[None], peak_value.reshape(1))


def solution(mesh):
    placed = (
        P("dp", ("seq", "tensor"), None),
        P(),
        P(("dp", "seq"), None, "tensor"),
        P(None, None, "tensor"),
        P(None, "tensor"),
        P("tensor"),
    )
    return jax.shard_map(
        shards,
        mesh=mesh,
        in_specs=placed,
        out_specs=(P("dp", "seq", "tensor"), P()),
        check_vma=False,
    )
```

profile of v0, /device:TPU:1, one launch (start us, length us, event | category | flops | bytes accessed | tf_op | source)
XLA Modules:
  0.0 297.4 jit_solution(4098233784942228399)
XLA Ops:
  7.2 1.6 fusion.5
  8.9 2.2 fusion.7
  11.0 0.0 all-gather.5.cloned.1.call-start
  11.1 0.7 abs_reduce_fusion
  11.8 83.3 %pmax.7 = f32[]{:T(128)} all-reduce(f32[]{:T(128)} %abs_reduce_fusion), channel_id=1, replica_groups=mesh['dp'=4,'seq'=8,'tensor'=8] {'dp','seq','tensor'}, use_global_device_ids=true, to_apply=%region_2.0 | all-reduce | flops 1 | bytes 8 | tf_op jit(solution)/shard_map/pmax | solution.py:55
  95.1 0.5 copy.13
  96.4 4.1 %multiply_convert_fusion = bf16[256,3,512]{0,2,1:T(8,128)(2,1)} fusion(f32[256,3,512]{0,2,1:T(8,128)S(1)} %copy.13, f32[]{:T(128)S(6)} %select_n.59), kind=kLoop, calls=%fused_computation.14 | loop fusion | flops 20840448 | bytes 2359300 | tf_op jit(solution)/shard_map/convert_element_type | solution.py:58
  100.6 10.0 %all-gather.3.cloned.1.call-done = bf16[1,512,8192]{2,1,0:T(8,128)(2,1)} async-done(((bf16[1,64,8192]{2,1,0:T(8,128)(2,1)}), bf16[1,512,8192]{2,1,0:T(8,128)(2,1)}) %all-gather.3.cloned.1.call-update) | async-done | bytes 8388624 | tf_op jit(solution)/shard_map/all_gather | solution.py:48
  110.6 109.6 %all-gather.5.cloned.1.call-done = bf16[8192,1536]{0,1:T(8,128)(2,1)} async-done(((bf16[256,1536]{0,1:T(8,128)(2,1)}), bf16[8192,1536]{0,1:T(8,128)(2,1)}) %all-gather.5.cloned.1.call-update) | async-done | bytes 25165840 | tf_op jit(solution)/shard_map/all_gather | solution.py:62
  220.2 19.4 %divide_convert_fusion = bf16[512,1536]{1,0:T(8,128)(2,1)S(1)} fusion(bf16[8192,1536]{0,1:T(8,128)(2,1)} %all-gather.5.cloned.1.call-done, bf16[1,512,8192]{2,1,0:T(8,128)(2,1)} %all-gather.3.cloned.1.call-done, f32[]{:T(128)S(6)} %select_n.59), kind=kOutput, calls=%fused_computation.3 | convolution fusion | flops 12886474752 | bytes 35127300 | tf_op jit(solution)/shard_map/dot_general | solution.py:60
  239.6 3.2 %collective-permute-start = (bf16[2,3,512]{2,1,0:T(4,128)(2,1)S(1)}, bf16[2,3,512]{2,1,0:T(4,128)(2,1)S(1)}, u32[]{:S(2)}, u32[]{:S(2)}) collective-permute-start(bf16[2,3,512]{2,1,0:T(4,128)(2,1)S(1)} %slice.39), channel_id=1, source_target_pairs={{0,8},{8,16},{16,24},{24,32},{32,40},{40,48},{48,56},{1,9},{9,17},... | collective-permute-start | bytes 18440 | tf_op jit(solution)/shard_map/ppermute | solution.py:15
  242.8 1.6 copy.14
  244.4 3.2 %copy.15 = bf16[512,3,512]{2,1,0:T(4,128)(2,1)S(1)} copy(bf16[512,3,512]{0,2,1:T(8,128)(2,1)} %bitcast.34) | data formatting | bytes 3145728 | tf_op jit(solution)/shard_map/reshape | solution.py:65
  247.6 5.1 %multiply_add_fusion = f32[512,3,512]{2,1,0:T(4,128)S(1)} fusion(bf16[512,3,512]{2,1,0:T(4,128)(2,1)S(1)} %copy.15, bf16[2,3,512]{2,1,0:T(4,128)(2,1)S(1)} %collective-permute-done, f32[3,512]{1,0:T(4,128)S(1)} %get-tuple-element.7, f32[3,512]{1,0:T(4,128)S(1)} %get-tuple-element.8, f32[3,512]{1,0:T(4,128)S(1)} %bitcast.39), kind=kLoop, calls=%fused_computation.2 | loop fusion | flops 7864320 | bytes 4743168 | tf_op jit(solution)/shard_map/add | solution.py:38
  252.7 1.9 copy-done
  254.7 1.6 fusion.13
  256.3 0.3 slice.54
  256.6 2.3 collective-permute-start.1
  259.0 0.2 rev.3
  259.2 0.1 copy.39
  259.3 1.4 collective-permute-done.1
  260.7 0.1 maximum_bitcast_fusion
  260.9 28.8 %fusion.15 = bf16[1,512,512]{2,0,1:T(2,128)(2,1)S(1)} fusion(f32[512,3,512]{2,1,0:T(4,128)} %copy-done, bf16[1,639,512]{2,1,0:T(8,128)(2,1)S(1)} %maximum_bitcast_fusion, bf16[512,1,512]{2,1,0:T(2,128)(2,1)S(1)} %fusion.13, f32[512]{0:T(512)S(1)} %copy-done.5, bf16[128,1,512]{2,0,1:T(8,128)(2,1)S(1)} %bitcast.38), kind=kOutput, calls=%fused_computation.31 | convolution fusion | flops 68419584 | bytes 2884608 | tf_op jit(solution)/shard_map/conv_general_dilated | solution.py:74
  289.7 0.9 copy.20
  (22 shorter events, 0.2 us)
Async XLA Ops:
  7.2 1.7 copy-start.2
  7.2 103.4 %all-gather.3.cloned.1.call-start = ((), (), s32[]{:S(2)}) async-start(), calls=%async_computation | async-start | bytes 9437184 | tf_op jit(solution)/shard_map/all_gather | solution.py:48
  8.9 2.2 copy-start.1
  11.0 209.1 %all-gather.5.cloned.1.call-start = ((), (), s32[]{:S(2)}) async-start(), calls=%async_computation.1 | async-start | bytes 25952256 | tf_op jit(solution)/shard_map/all_gather | solution.py:62
  96.4 4.1 %copy-start.4 = (f32[3,3,512]{2,1,0:T(4,128)S(1)}, f32[3,3,512]{2,1,0:T(4,128)}, u32[]{:S(2)}) copy-start(f32[3,3,512]{2,1,0:T(4,128)} %param.9) | copy-start | bytes 55300
  239.6 8.1 %collective-permute-start = (bf16[2,3,512]{2,1,0:T(4,128)(2,1)S(1)}, bf16[2,3,512]{2,1,0:T(4,128)(2,1)S(1)}, u32[]{:S(2)}, u32[]{:S(2)}) collective-permute-start(bf16[2,3,512]{2,1,0:T(4,128)(2,1)S(1)} %slice.39), channel_id=1, source_target_pairs={{0,8},{8,16},{16,24},{24,32},{32,40},{40,48},{48,56},{1,9},{9,17},... | collective-permute-start | bytes 18440 | tf_op jit(solution)/shard_map/ppermute | solution.py:15
  252.7 1.9 copy-start
  254.7 4.3 %copy-start.3 = (bf16[128,512]{1,0:T(8,128)(2,1)S(1)}, bf16[128,512]{1,0:T(8,128)(2,1)}, u32[]{:S(2)}) copy-start(bf16[128,512]{1,0:T(8,128)(2,1)} %param.10) | copy-start | bytes 393220
  256.6 4.2 %copy-start.5 = (f32[512]{0:T(512)S(1)}, f32[512]{0:T(512)}, u32[]{:S(2)}) copy-start(f32[512]{0:T(512)} %param.11) | copy-start | bytes 6148
  256.6 4.1 %collective-permute-start.1 = (bf16[127,512]{1,0:T(8,128)(2,1)S(1)}, bf16[127,512]{1,0:T(8,128)(2,1)S(1)}, u32[]{:S(2)}, u32[]{:S(2)}) collective-permute-start(bf16[127,512]{1,0:T(8,128)(2,1)S(1)} %bitcast.37), channel_id=1, source_target_pairs={{0,8},{8,16},{16,24},{24,32},{32,40},{40,48},{48,56},{1,9},{9,17},... | collective-permute-start | bytes 390152 | tf_op jit(solution)/shard_map/ppermute | solution.py:15
Sparse Core Ops, SparseCore 0:
  11.2 99.3 all-gather.2
  113.0 107.0 all-gather.4
where the time goes:
time: 298 us; the launch traced here: 297 us
  waiting for transfers between devices  121 us (41%)
  blocking collectives  83.3 us (28%)
  matrix products  48.1 us (16%)
  other arithmetic  15.4 us (5%)
  between operations  15.1 us (5%)
  local copies, waits for them, and re-layouts  8.8 us (3%)
  starting transfers between devices  5.61 us (2%)
    all_gather x1, waiting for transfers between devices, shards(): lax.all_gather(recast, ('dp', 'seq'), axis=0, tiled=True)  110 us
    pmax x1, blocking collectives, shards(): lax.pmax(jnp.max(jnp.abs(master_weight)), ('dp', 'seq', 'tensor'))  83.3 us
    conv_general_dilated x1, matrix products, shards(): lax.conv_general_dilated(extended[None], kernel, (1,), 'VALID', dimension...  28.8 us
    dot_general x1, matrix products, shards(): jnp.dot(flat_rows, lax.all_gather(recast, ('dp', 'seq'), axis=0, tiled=Tr...  19.4 us
    all_gather x1, waiting for transfers between devices, shards(): gathered = lax.all_gather(normed, 'tensor', axis=1, tiled=True)  9.99 us
  transfers between devices with their start and end apart: 4, of which 3 were waited for; matrix products, arithmetic and copies ran while one was open for 4% of the time, Pallas kernels for 0%

commit v1 on v0

--- a/solution.py
+++ b/solution.py
@@ -45,7 +45,9 @@
     values = tokens.astype(jnp.float32)
     square_mean = jnp.mean(values * values, axis=-1, keepdims=True)
     normed = (values * lax.rsqrt(square_mean + eps_norm) * norm_gain).astype(jnp.bfloat16)
-    gathered = lax.all_gather(normed, "tensor", axis=1, tiled=True)
+    gathered = jnp.concatenate(
+        lax.all_to_all(jnp.stack([normed] * lax.axis_size("tensor")), "tensor", 0, 0), axis=1
+    )
     stacks = gathered.shape[0]
     seq_rows = gathered.shape[1]
     model_width = gathered.shape[2]

time: 298 us -> 370 us (1.24)
  waiting for transfers between devices: 121 us -> 188 us
  local copies, waits for them, and re-layouts: 8.8 us -> 13 us
    all_to_all x0 -> x1, waiting for transfers between devices: none -> 187 us  [shards(): lax.all_to_all(jnp.stack([normed] * lax.axis_size('tensor')), 'tensor', 0...]
    all_gather x1, waiting for transfers between devices: 110 us -> 0.01 us  [shards(): lax.all_gather(recast, ('dp', 'seq'), axis=0, tiled=True)]
    all_gather x1 -> x0, waiting for transfers between devices: 9.99 us -> none  [shards(): gathered = lax.all_gather(normed, 'tensor', axis=1, tiled=True)]
    all_to_all x0 -> x1, starting transfers between devices: none -> 5.24 us  [shards(): lax.all_to_all(jnp.stack([normed] * lax.axis_size('tensor')), 'tensor', 0...]
    another operation x0 -> x1, local copies, waits for them, and re-layouts: none -> 4.23 us  [shards(): jnp.stack([normed] * lax.axis_size('tensor'))]
  transfers between devices with their start and end apart: 4 -> 4, of which waited for: 3 -> 2; matrix products, arithmetic and copies ran while one was open for 4% -> 3% of each run, Pallas kernels for 0% -> 0%
where the time goes in v1:
time: 370 us; the launch traced here: 369 us
  waiting for transfers between devices  188 us (51%)
  blocking collectives  81.4 us (22%)
  matrix products  48.1 us (13%)
  between operations  15.1 us (4%)
  other arithmetic  13.8 us (4%)
  local copies, waits for them, and re-layouts  13 us (4%)
  starting transfers between devices  9.29 us (3%)
    all_to_all x1, waiting for transfers between devices, shards(): lax.all_to_all(jnp.stack([normed] * lax.axis_size('tensor')), 'tensor', 0...  187 us
    pmax x1, blocking collectives, shards(): lax.pmax(jnp.max(jnp.abs(master_weight)), ('dp', 'seq', 'tensor'))  81.4 us
    conv_general_dilated x1, matrix products, shards(): lax.conv_general_dilated(extended[None], kernel, (1,), 'VALID', dimension...  28.8 us
    dot_general x1, matrix products, shards(): jnp.dot(flat_rows, lax.all_gather(recast, ('dp', 'seq'), axis=0, tiled=Tr...  19.4 us
  transfers between devices with their start and end apart: 4, of which 2 were waited for; matrix products, arithmetic and copies ran while one was open for 3% of the time, Pallas kernels for 0%

profile of v1, /device:TPU:1, one launch (start us, length us, event | category | flops | bytes accessed | tf_op | source)
XLA Modules:
  0.0 369.2 jit_solution(15589493449532044480)
XLA Ops:
  7.2 2.3 abs_reduce_fusion
  9.5 0.5 copy.13
  10.0 81.4 %pmax.7 = f32[]{:T(128)} all-reduce(f32[]{:T(128)} %abs_reduce_fusion), channel_id=1, replica_groups=mesh['dp'=4,'seq'=8,'tensor'=8] {'dp','seq','tensor'}, use_global_device_ids=true, to_apply=%region_2.0 | all-reduce | flops 1 | bytes 8 | tf_op jit(solution)/shard_map/pmax | solution.py:57
  92.2 4.1 %multiply_convert_fusion = bf16[256,3,512]{0,2,1:T(8,128)(2,1)} fusion(f32[256,3,512]{0,2,1:T(8,128)S(1)} %copy.13, f32[]{:T(128)S(6)} %select_n.59), kind=kLoop, calls=%fused_computation.12 | loop fusion | flops 20840448 | bytes 2359300 | tf_op jit(solution)/shard_map/convert_element_type | solution.py:60
  96.3 0.3 fusion.1
  96.6 0.3 fusion.9
  96.9 4.2 %stack.2 = bf16[8,1,64,8192]{3,2,1,0:T(8,128)(2,1)} broadcast(bf16[64,8192]{1,0:T(8,128)(2,1)S(1)} %fusion.9), dimensions={2,3} | broadcast | bytes 9437184 | tf_op jit(solution)/shard_map/stack | solution.py:49
  101.2 5.2 %all-to-all-start = ((bf16[8,1,64,8192]{3,2,1,0:T(8,128)(2,1)}), bf16[8,1,64,8192]{3,2,1,0:T(8,128)(2,1)}, u32[]{:S(2)}, u32[]{:S(2)}) async-start(bf16[8,1,64,8192]{3,2,1,0:T(8,128)(2,1)} %stack.2), calls=%async_computation | async-start | bytes 16777216 | tf_op jit(solution)/shard_map/all_to_all | solution.py:49
  106.4 186.8 %all-to-all-done = bf16[8,1,64,8192]{3,2,1,0:T(8,128)(2,1)} async-done(((bf16[8,1,64,8192]{3,2,1,0:T(8,128)(2,1)}), bf16[8,1,64,8192]{3,2,1,0:T(8,128)(2,1)}, u32[]{:S(2)}, u32[]{:S(2)}) %all-to-all-start) | async-done | bytes 8388640 | tf_op jit(solution)/shard_map/all_to_all | solution.py:49
  293.3 19.4 %divide_convert_fusion = bf16[512,1536]{1,0:T(8,128)(2,1)S(1)} fusion(bf16[512,8192]{1,0:T(8,128)(2,1)} %bitcast.1, bf16[8192,1536]{0,1:T(8,128)(2,1)} %all-gather.2.cloned.1.call-done, f32[]{:T(128)S(6)} %select_n.59), kind=kOutput, calls=%fused_computation.1 | convolution fusion | flops 12886474752 | bytes 35127300 | tf_op jit(solution)/shard_map/dot_general | solution.py:62
  312.7 2.1 collective-permute-start
  314.8 1.6 copy.14
  316.4 3.2 copy.15
  319.7 5.1 %multiply_add_fusion = f32[512,3,512]{2,1,0:T(4,128)S(1)} fusion(bf16[512,3,512]{2,1,0:T(4,128)(2,1)S(1)} %copy.15, bf16[2,3,512]{2,1,0:T(4,128)(2,1)S(1)} %collective-permute-done, f32[3,512]{1,0:T(4,128)S(1)} %get-tuple-element.7, f32[3,512]{1,0:T(4,128)S(1)} %get-tuple-element.8, f32[3,512]{1,0:T(4,128)S(1)} %bitcast.38), kind=kLoop, calls=%fused_computation | loop fusion | flops 7864320 | bytes 4743168 | tf_op jit(solution)/shard_map/add | solution.py:38
  324.8 1.9 copy-done
  326.7 1.6 fusion.10
  328.4 0.3 slice.54
  328.7 1.9 collective-permute-start.1
  330.6 0.2 rev.3
  330.8 0.1 copy.39
  330.9 1.6 collective-permute-done.1
  332.5 0.1 maximum_bitcast_fusion
  332.7 28.8 %fusion.12 = bf16[1,512,512]{2,0,1:T(2,128)(2,1)S(1)} fusion(f32[512,3,512]{2,1,0:T(4,128)} %copy-done, bf16[1,639,512]{2,1,0:T(8,128)(2,1)S(1)} %maximum_bitcast_fusion, bf16[512,1,512]{2,1,0:T(2,128)(2,1)S(1)} %fusion.10, f32[512]{0:T(512)S(1)} %copy-done.6, bf16[128,1,512]{2,0,1:T(8,128)(2,1)S(1)} %bitcast.37), kind=kOutput, calls=%fused_computation.30 | convolution fusion | flops 68419584 | bytes 2884608 | tf_op jit(solution)/shard_map/conv_general_dilated | solution.py:76
  361.5 0.9 copy.20
  (24 shorter events, 0.2 us)
Async XLA Ops:
  7.2 2.3 copy-start.1
  7.2 286.1 %all-gather.2.cloned.1.call-start = ((), (), s32[]{:S(2)}) async-start(), calls=%async_computation.1 | async-start | bytes 25952256 | tf_op jit(solution)/shard_map/all_gather | solution.py:64
  92.2 4.1 %copy-start.2 = (bf16[1,64,8192]{2,1,0:T(8,128)(2,1)S(1)}, bf16[1,64,8192]{2,1,0:T(8,128)(2,1)}, u32[]{:S(2)}) copy-start(bf16[1,64,8192]{2,1,0:T(8,128)(2,1)} %param.6) | copy-start | bytes 3145732
  92.2 4.4 %copy-start.4 = (f32[8192]{0:T(1024)S(1)}, f32[8192]{0:T(1024)}, u32[]{:S(2)}) copy-start(f32[8192]{0:T(1024)} %param.7) | copy-start | bytes 98308
  101.2 5.2 %copy-start.5 = (f32[3,3,512]{2,1,0:T(4,128)S(1)}, f32[3,3,512]{2,1,0:T(4,128)}, u32[]{:S(2)}) copy-start(f32[3,3,512]{2,1,0:T(4,128)} %param.9) | copy-start | bytes 55300
  101.2 192.1 %all-to-all-start = ((bf16[8,1,64,8192]{3,2,1,0:T(8,128)(2,1)}), bf16[8,1,64,8192]{3,2,1,0:T(8,128)(2,1)}, u32[]{:S(2)}, u32[]{:S(2)}) async-start(bf16[8,1,64,8192]{3,2,1,0:T(8,128)(2,1)} %stack.2), calls=%async_computation | async-start | bytes 16777216 | tf_op jit(solution)/shard_map/all_to_all | solution.py:49
  312.7 7.0 %collective-permute-start = (bf16[2,3,512]{2,1,0:T(4,128)(2,1)S(1)}, bf16[2,3,512]{2,1,0:T(4,128)(2,1)S(1)}, u32[]{:S(2)}, u32[]{:S(2)}) collective-permute-start(bf16[2,3,512]{2,1,0:T(4,128)(2,1)S(1)} %slice.39), channel_id=1, source_target_pairs={{0,8},{8,16},{16,24},{24,32},{32,40},{40,48},{48,56},{1,9},{9,17},... | collective-permute-start | bytes 18440 | tf_op jit(solution)/shard_map/ppermute | solution.py:15
  324.8 1.9 copy-start
  326.7 3.9 %copy-start.3 = (bf16[128,512]{1,0:T(8,128)(2,1)S(1)}, bf16[128,512]{1,0:T(8,128)(2,1)}, u32[]{:S(2)}) copy-start(bf16[128,512]{1,0:T(8,128)(2,1)} %param.10) | copy-start | bytes 393220
  328.7 4.0 %copy-start.6 = (f32[512]{0:T(512)S(1)}, f32[512]{0:T(512)}, u32[]{:S(2)}) copy-start(f32[512]{0:T(512)} %param.11) | copy-start | bytes 6148
  328.7 3.9 %collective-permute-start.1 = (bf16[127,512]{1,0:T(8,128)(2,1)S(1)}, bf16[127,512]{1,0:T(8,128)(2,1)S(1)}, u32[]{:S(2)}, u32[]{:S(2)}) collective-permute-start(bf16[127,512]{1,0:T(8,128)(2,1)S(1)} %bitcast.36), channel_id=1, source_target_pairs={{0,8},{8,16},{16,24},{24,32},{32,40},{40,48},{48,56},{1,9},{9,17},... | collective-permute-start | bytes 390152 | tf_op jit(solution)/shard_map/ppermute | solution.py:15
Sparse Core Ops, SparseCore 0:
  96.4 103.7 all-gather.1
